TPU v7x, 32 devices: a whole 2x2x4 slice. The times are simulated.
32 devices in a mesh: dp: 8 (over y, x, core), tensor: 4 (over z).
Axes of the slice: x: 2, y: 2, z: 4, core: 2. Of those that a mesh axis runs over, the one named last changes fastest.
Arguments:
- tokens: bfloat16 [6144, 2048], P(('dp', 'tensor')), may hold values from -6 to 6
- cotangent: bfloat16 [6144, 2048], P(('dp', 'tensor')), may hold values from -6 to 6
- deal: int32 [6144], P(('dp', 'tensor')), may hold values from 0 to 6143, as said below
- segment: int32 [6144], P('dp'), may hold values from 0 to 3, as said below
- norm1_gain: float32 [2, 2048], replicated, may hold values from 0.5 to 1.5
- norm1_shift: float32 [2, 2048], replicated, may hold values from -1.25 to 1.25
- query_weight: bfloat16 [2, 2048, 2048], P(None, 'dp', 'tensor'), may hold values from -0.125 to 0.125
- query_bias: float32 [2, 2048], P(None, 'tensor'), may hold values from -3 to 3
- kv_weight: bfloat16 [2, 2048, 256], P(None, 'dp', 'tensor'), may hold values from -0.125 to 0.125
- value_bias: float32 [2, 128], replicated, may hold values from -0.3125 to 0.3125
- out_weight: bfloat16 [2, 2048, 2048], P(None, 'tensor', 'dp'), may hold values from -1.5 to 1.5
- out_bias: float32 [2, 2048], replicated, may hold values from -1.75 to 1.75
- norm2_gain: float32 [2, 2048], replicated, may hold values from 0.5 to 1.5
- norm2_shift: float32 [2, 2048], replicated, may hold values from -1.25 to 1.25
- up_weight: bfloat16 [2, 2048, 8192], P(None, 'dp', 'tensor'), may hold values from -0.125 to 0.125
- up_bias: float32 [2, 8192], P(None, 'tensor'), may hold values from -3 to 3
- down_weight: bfloat16 [2, 8192, 2048], P(None, 'tensor', 'dp'), may hold values from -0.0625 to 0.0625
- down_bias: float32 [2, 2048], replicated, may hold values from -1.75 to 1.75
Outputs:
- layer_out: bfloat16 [6144, 2048], P(('dp', 'tensor'))
- tokens_grad: bfloat16 [6144, 2048], P(('dp', 'tensor'))
- norm1_gain_grad: float32 [2, 2048], replicated
- norm1_shift_grad: float32 [2, 2048], replicated
- query_weight_grad: float32 [2, 2048, 2048], P(None, 'dp', 'tensor')
- query_bias_grad: float32 [2, 2048], P(None, 'tensor')
- kv_weight_grad: float32 [2, 2048, 256], P(None, 'dp', 'tensor')
- value_bias_grad: float32 [2, 128], replicated
- out_weight_grad: float32 [2, 2048, 2048], P(None, 'tensor', 'dp')
- out_bias_grad: float32 [2, 2048], replicated
- norm2_gain_grad: float32 [2, 2048], replicated
- norm2_shift_grad: float32 [2, 2048], replicated
- up_weight_grad: float32 [2, 2048, 8192], P(None, 'dp', 'tensor')
- up_bias_grad: float32 [2, 8192], P(None, 'tensor')
- down_weight_grad: float32 [2, 8192, 2048], P(None, 'tensor', 'dp')
- down_bias_grad: float32 [2, 2048], replicated
Inputs may be any that keep to these rules, and one draw needn't show every extreme that they name: deal is a permutation: input row i becomes working row deal[i]; rows of both orders are laid out over the devices in order, 192 a device; a row stays on a device of the same tensor index, and every device deals exactly 24 rows to each dp index. `segment`: within each group of 768 working rows the labels never fall; each run of equal labels is one sequence of 96 to 768 rows; the first group is one sequence of all its rows.
All inputs are finite; a program needn't handle non-finite values.
Results may differ from a plain program's by a relative error of at most 0.025.
Values may be sent and summed in bfloat16 or wider, within the bound.
No kernel may reach another device: no remote copies, remote signals or barrier semaphores. Data moves between devices by JAX's collectives and lax.ppermute only.
A program may use at most 256 MiB of HBM per device.

v0:
```python
import jax
import jax.numpy as jnp
from jax import lax
from jax.sharding import PartitionSpec as P

HEAD = 128
EPSILON = 1e-05


def layer_norm(values, scales, offsets):
    row_mean = jnp.mean(values, axis=-1, keepdims=True)
    centred = values - row_mean
    row_var = jnp.mean(centred * centred, axis=-1, keepdims=True)
    return centred * lax.rsqrt(row_var + EPSILON) * scales + offsets


def gelu_tanh(values):
    return jax.nn.gelu(values, approximate=True)


def matmul(left, right):
    return jnp.dot(left, right, preferred_element_type=jnp.float32)


def contract_rows(left, right):
    return lax.dot_general(
        left, right, (((0,), (0,)), ((), ())), preferred_element_type=jnp.float32
    )


def contract_cols(left, right):
    return lax.dot_general(
        left, right, (((1,), (1,)), ((), ())), preferred_element_type=jnp.float32
    )


def rows_gather(values):
    return lax.all_gather(values, "tensor", axis=0, tiled=True)


def grad_gather(values):
    return lax.all_gather(values, "tensor", axis=0, tiled=True)


def rows_scatter(left, right):
    return lax.psum_scatter(
        matmul(left, right).astype(jnp.bfloat16), "tensor", scatter_dimension=0, tiled=True
    ).astype(jnp.float32)


def grad_scatter(factor_pairs):
    running = None
    for gradient, weight in factor_pairs:
        product_piece = contract_cols(gradient, weight)
        running = product_piece if running is None else running + product_piece
    return lax.psum_scatter(
        running.astype(jnp.bfloat16), "tensor", scatter_dimension=0, tiled=True
    ).astype(jnp.float32)


def place_slice(values, full_width, tensor_rank):
    start_col = tensor_rank * values.shape[0]
    return lax.dynamic_update_slice(jnp.zeros((full_width,), jnp.float32), values, (start_col,))


def local(
    tokens,
    cotangent,
    deal,
    segment,
    norm1_gain,
    norm1_shift,
    query_weight,
    query_bias,
    kv_weight,
    value_bias,
    out_weight,
    out_bias,
    norm2_gain,
    norm2_shift,
    up_weight,
    up_bias,
    down_weight,
    down_bias,
):
    local_rows = tokens.shape[0]
    dp_count = lax.axis_size("dp")
    tensor_count = lax.axis_size("tensor")
    tensor_rank = lax.axis_index("tensor")
    slot_rows = local_rows // dp_count
    layer_total = query_weight.shape[0]
    group_rows = local_rows * tensor_count
    query_cols = query_weight.shape[2]
    pair_width = kv_weight.shape[2]
    hidden_cols = up_weight.shape[2]
    head_count = query_cols // HEAD
    score_scale = HEAD ** (-0.5)
    target_dev = deal // local_rows // tensor_count
    target_row = deal % local_rows
    dev_ids = jnp.arange(dp_count, dtype=jnp.int32)
    dev_match = (target_dev[:, None] == dev_ids[None, :]).astype(jnp.int32)
    earlier = jnp.cumsum(dev_match, axis=0) - dev_match
    slot_of = target_dev * slot_rows + jnp.sum(earlier * dev_match, axis=1)
    row_ids = jnp.arange(local_rows, dtype=jnp.int32)
    send_mask = row_ids[:, None] == slot_of[None, :]
    send_table = send_mask.astype(jnp.bfloat16)
    sent_place = jnp.sum(jnp.where(send_mask, target_row[None, :], 0), axis=1)
    arrived_place = lax.all_to_all(sent_place, "dp", split_axis=0, concat_axis=0, tiled=True)
    tokens_sent = matmul(send_table, tokens).astype(jnp.bfloat16)
    tangent_sent = matmul(send_table, cotangent).astype(jnp.bfloat16)
    tokens_come, tangent_come = (
        lax.all_to_all(tokens_sent, "dp", split_axis=0, concat_axis=0, tiled=True),
        lax.all_to_all(tangent_sent, "dp", split_axis=0, concat_axis=0, tiled=True),
    )
    place_table = (row_ids[:, None] == arrived_place[None, :]).astype(jnp.bfloat16)
    stream = matmul(place_table, tokens_come)
    tangent = matmul(place_table, tangent_come)
    places = jnp.arange(group_rows, dtype=jnp.int32)
    allowed = (places[None, :] <= places[:, None]) & (segment[:, None] == segment[None, :])
    saved = []
    kept_weights = []
    for layer_index in range(layer_total):
        w_query, w_pair, w_out, w_up, w_down = (
            lax.all_gather(query_weight[layer_index], "dp", axis=0, tiled=True),
            lax.all_gather(kv_weight[layer_index], "dp", axis=0, tiled=True),
            lax.all_gather(out_weight[layer_index], "dp", axis=1, tiled=True),
            lax.all_gather(up_weight[layer_index], "dp", axis=0, tiled=True),
            lax.all_gather(down_weight[layer_index], "dp", axis=1, tiled=True),
        )
        kept_weights.append(None)
        normed_one = layer_norm(stream, norm1_gain[layer_index], norm1_shift[layer_index]).astype(
            jnp.bfloat16
        )
        normed_all = rows_gather(normed_one)
        queries = (matmul(normed_all, w_query) + query_bias[layer_index]).astype(jnp.bfloat16)
        full_bias = jnp.concatenate([jnp.zeros((HEAD,), jnp.float32), value_bias[layer_index]])
        pair_bias = lax.dynamic_slice_in_dim(full_bias, tensor_rank * pair_width, pair_width)
        pair_local = (matmul(normed_all, w_pair) + pair_bias).astype(jnp.bfloat16)
        pair_all = lax.all_gather(pair_local, "tensor", axis=1, tiled=True)
        key_rows = pair_all[:, :HEAD]
        value_rows = pair_all[:, HEAD:]
        query_heads = jnp.transpose(queries.reshape(group_rows, head_count, HEAD), (1, 0, 2))

        def attend(query_one):
            scores = jnp.where(allowed, contract_cols(query_one, key_rows) * score_scale, -1e30)
            row_top = jnp.max(scores, axis=-1, keepdims=True)
            exp_score = jnp.exp(scores - row_top)
            row_total = jnp.sum(exp_score, axis=-1, keepdims=True)
            weights = (exp_score / row_total).astype(jnp.bfloat16)
            return (matmul(weights, value_rows), (row_top + jnp.log(row_total))[:, 0])

        head_outs, log_totals = lax.map(attend, query_heads)
        mixed = (
            jnp.transpose(head_outs, (1, 0, 2)).reshape(group_rows, query_cols).astype(jnp.bfloat16)
        )
        hidden_state = stream + rows_scatter(mixed, w_out) + out_bias[layer_index]
        normed_two = layer_norm(
            hidden_state, norm2_gain[layer_index], norm2_shift[layer_index]
        ).astype(jnp.bfloat16)
        normed_two_all = rows_gather(normed_two)
        pre_gelu = matmul(normed_two_all, w_up) + up_bias[layer_index]
        activation = gelu_tanh(pre_gelu).astype(jnp.bfloat16)
        saved.append(
            (
                stream,
                normed_all,
                queries,
                pair_all,
                log_totals,
                mixed,
                hidden_state,
                normed_two_all,
                pre_gelu,
                activation,
            )
        )
        stream = hidden_state + rows_scatter(activation, w_down) + down_bias[layer_index]
    layer_out = stream.astype(jnp.bfloat16)
    reduced_by_layer = [None] * layer_total
    small_by_layer = [None] * layer_total
    for layer_index in reversed(range(layer_total)):
        (
            stream_in,
            normed_all,
            queries,
            pair_all,
            log_totals,
            mixed,
            hidden_state,
            normed_two_all,
            pre_gelu,
            activation,
        ) = saved[layer_index]
        w_query, w_pair, w_out, w_up, w_down = (
            lax.all_gather(query_weight[layer_index], "dp", axis=0, tiled=True),
            lax.all_gather(kv_weight[layer_index], "dp", axis=0, tiled=True),
            lax.all_gather(out_weight[layer_index], "dp", axis=1, tiled=True),
            lax.all_gather(up_weight[layer_index], "dp", axis=0, tiled=True),
            lax.all_gather(down_weight[layer_index], "dp", axis=1, tiled=True),
        )
        key_rows = pair_all[:, :HEAD]
        value_rows = pair_all[:, HEAD:]
        branch_grad = tangent.astype(jnp.bfloat16)
        down_bias_part = jnp.sum(branch_grad.astype(jnp.float32), axis=0)
        branch_all = grad_gather(branch_grad)
        down_grad = contract_rows(activation, branch_all)
        act_grad = contract_cols(branch_all, w_down)
        pre_grad = jax.vjp(gelu_tanh, pre_gelu)[1](act_grad)[0].astype(jnp.bfloat16)
        up_bias_part = jnp.sum(pre_grad.astype(jnp.float32), axis=0)
        up_grad = contract_rows(normed_two_all, pre_grad)
        normed_two_grad = grad_scatter(((pre_grad, w_up),))
        norm_pull_two = jax.vjp(
            layer_norm, hidden_state, norm2_gain[layer_index], norm2_shift[layer_index]
        )[1]
        hidden_part, gain_two_part, shift_two_part = norm_pull_two(normed_two_grad)
        hidden_grad = tangent + hidden_part
        attn_grad = hidden_grad.astype(jnp.bfloat16)
        out_bias_part = jnp.sum(attn_grad.astype(jnp.float32), axis=0)
        attn_all = grad_gather(attn_grad)
        out_grad = contract_rows(mixed, attn_all)
        mixed_grad = contract_cols(attn_all, w_out).astype(jnp.bfloat16)
        query_heads = jnp.transpose(queries.reshape(group_rows, head_count, HEAD), (1, 0, 2))
        dout_heads = jnp.transpose(mixed_grad.reshape(group_rows, head_count, HEAD), (1, 0, 2))

        def attend_back(carried, inputs):
            query_one, dout_one, log_one = inputs
            scores = jnp.where(allowed, contract_cols(query_one, key_rows) * score_scale, -1e30)
            probs = jnp.exp(scores - log_one[:, None])
            prob_grad = contract_cols(dout_one, value_rows)
            inner = jnp.sum(probs * prob_grad, axis=-1, keepdims=True)
            score_grad = (probs * (prob_grad - inner) * score_scale).astype(jnp.bfloat16)
            key_acc = carried[0] + contract_rows(score_grad, query_one)
            value_acc = carried[1] + contract_rows(probs.astype(jnp.bfloat16), dout_one)
            return ((key_acc, value_acc), matmul(score_grad, key_rows))

        start_acc = (
            jnp.zeros((group_rows, HEAD), jnp.float32),
            jnp.zeros((group_rows, HEAD), jnp.float32),
        )
        (key_grad, value_grad), query_grads = lax.scan(
            attend_back, start_acc, (query_heads, dout_heads, log_totals)
        )
        query_grad = (
            jnp.transpose(query_grads, (1, 0, 2))
            .reshape(group_rows, query_cols)
            .astype(jnp.bfloat16)
        )
        query_bias_part = jnp.sum(query_grad.astype(jnp.float32), axis=0)
        pair_part = jnp.concatenate([key_grad, value_grad], axis=1)
        pair_grad = lax.psum_scatter(
            pair_part.astype(jnp.bfloat16), "tensor", scatter_dimension=1, tiled=True
        )
        pair_bias_part = jnp.sum(pair_grad.astype(jnp.float32), axis=0)
        query_w_grad = contract_rows(normed_all, query_grad)
        pair_w_grad = contract_rows(normed_all, pair_grad)
        normed_grad = grad_scatter(((query_grad, w_query), (pair_grad, w_pair)))
        norm_pull_one = jax.vjp(
            layer_norm, stream_in, norm1_gain[layer_index], norm1_shift[layer_index]
        )[1]
        stream_part, gain_one_part, shift_one_part = norm_pull_one(normed_grad)
        tangent = hidden_grad + stream_part
        small_by_layer[layer_index] = (
            gain_one_part,
            shift_one_part,
            place_slice(query_bias_part, query_cols * tensor_count, tensor_rank),
            place_slice(pair_bias_part, pair_width * tensor_count, tensor_rank),
            out_bias_part,
            gain_two_part,
            shift_two_part,
            place_slice(up_bias_part, hidden_cols * tensor_count, tensor_rank),
            down_bias_part,
        )
        reduced_by_layer[layer_index] = (
            lax.psum_scatter(
                query_w_grad.astype(jnp.bfloat16), "dp", scatter_dimension=0, tiled=True
            ).astype(jnp.float32),
            lax.psum_scatter(
                pair_w_grad.astype(jnp.bfloat16), "dp", scatter_dimension=0, tiled=True
            ).astype(jnp.float32),
            lax.psum_scatter(
                out_grad.astype(jnp.bfloat16), "dp", scatter_dimension=1, tiled=True
            ).astype(jnp.float32),
            lax.psum_scatter(
                up_grad.astype(jnp.bfloat16), "dp", scatter_dimension=0, tiled=True
            ).astype(jnp.float32),
            lax.psum_scatter(
                down_grad.astype(jnp.bfloat16), "dp", scatter_dimension=1, tiled=True
            ).astype(jnp.float32),
        )
    summed = [
        jnp.stack([reduced_by_layer[layer_index][member] for layer_index in range(layer_total)])
        for member in range(5)
    ]
    smalls = [
        jnp.stack([small_by_layer[layer_index][member] for layer_index in range(layer_total)])
        for member in range(9)
    ]
    (
        gain_one_sum,
        shift_one_sum,
        query_bias_sum,
        pair_bias_sum,
        out_bias_sum,
        gain_two_sum,
        shift_two_sum,
        up_bias_sum,
        down_bias_sum,
    ) = lax.psum(
        (
            smalls[0],
            smalls[1],
            smalls[2],
            smalls[3],
            smalls[4],
            smalls[5],
            smalls[6],
            smalls[7],
            smalls[8],
        ),
        ("dp", "tensor"),
    )
    query_bias_grad = lax.dynamic_slice_in_dim(
        query_bias_sum, tensor_rank * query_cols, query_cols, 1
    )
    up_bias_grad = lax.dynamic_slice_in_dim(up_bias_sum, tensor_rank * hidden_cols, hidden_cols, 1)
    value_bias_grad = pair_bias_sum[:, HEAD:]
    out_slots = contract_rows(place_table, layer_out).astype(jnp.bfloat16)
    grad_slots = contract_rows(place_table, tangent.astype(jnp.bfloat16)).astype(jnp.bfloat16)
    out_back, grad_back = (
        lax.all_to_all(out_slots, "dp", split_axis=0, concat_axis=0, tiled=True),
        lax.all_to_all(grad_slots, "dp", split_axis=0, concat_axis=0, tiled=True),
    )
    layer_rows = contract_rows(send_table, out_back).astype(jnp.bfloat16)
    token_rows = contract_rows(send_table, grad_back).astype(jnp.bfloat16)
    return (
        layer_rows,
        token_rows,
        gain_one_sum,
        shift_one_sum,
        summed[0],
        query_bias_grad,
        summed[1],
        value_bias_grad,
        summed[2],
        out_bias_sum,
        gain_two_sum,
        shift_two_sum,
        summed[3],
        up_bias_grad,
        summed[4],
        down_bias_sum,
    )


def solution(mesh):
    in_specs = (
        P(("dp", "tensor"), None),
        P(("dp", "tensor"), None),
        P(("dp", "tensor")),
        P("dp"),
        P(),
        P(),
        P(None, "dp", "tensor"),
        P(None, "tensor"),
        P(None, "dp", "tensor"),
        P(),
        P(None, "tensor", "dp"),
        P(),
        P(),
        P(),
        P(None, "dp", "tensor"),
        P(None, "tensor"),
        P(None, "tensor", "dp"),
        P(),
    )
    out_specs = (
        P(("dp", "tensor"), None),
        P(("dp", "tensor"), None),
        P(),
        P(),
        P(None, "dp", "tensor"),
        P(None, "tensor"),
        P(None, "dp", "tensor"),
        P(),
        P(None, "tensor", "dp"),
        P(),
        P(),
        P(),
        P(None, "dp", "tensor"),
        P(None, "tensor"),
        P(None, "tensor", "dp"),
        P(),
    )
    return jax.shard_map(local, mesh=mesh, in_specs=in_specs, out_specs=out_specs, check_vma=False)
```

profile of v0, /device:TPU:0, one launch (start us, length us, event | category | flops | bytes accessed | tf_op | source)
XLA Modules:
  0.0 2494.6 jit_solution(4482688082752972419)
XLA Ops:
  50.9 50.5 %all-gather.27.cloned.1.call-done = bf16[768,2048]{1,0:T(8,128)(2,1)} async-done(((bf16[192,2048]{1,0:T(8,128)(2,1)}), bf16[768,2048]{1,0:T(8,128)(2,1)}) %all-gather.27.cloned.1.call-update) | async-done | bytes 3145744 | tf_op jit(solution)/shard_map/all_gather | solution.py:38
  104.3 15.1 all_gather.73
  135.8 34.1 %while.56 = (s32[]{:T(128)}, bf16[4,768,128]{1,2,0:T(8,128)(2,1)S(1)}, f32[4,768]{1,0:T(4,128)}, bf16[4,768,128]{2,1,0:T(8,128)(2,1)S(1)}, bf16[768,128]{1,0:T(8...) while((s32[]{:T(128)}, ...), condition=%wide.region_9.10_spmd.clone, body=%wide.region_6.9_spmd.clone.sunk | while | flops 308477184 | bytes 8108645 | solution.py:152
  179.2 56.9 %reduce-scatter.25.cloned.1.call-done = bf16[192,2048]{1,0:T(8,128)(2,1)} async-done(((bf16[768,2048]{1,0:T(8,128)(2,1)}), bf16[192,2048]{1,0:T(8,128)(2,1)}) %reduce-scatter.25.cloned.1.call-update) | async-done | bytes 786448 | tf_op jit(solution)/shard_map/reduce_scatter | solution.py:46
  242.8 50.0 %all-gather.47.cloned.1.call-done = bf16[1,2048,2048]{2,1,0:T(8,128)(2,1)} async-done(((bf16[1,256,2048]{2,1,0:T(8,128)(2,1)}), bf16[1,2048,2048]{2,1,0:T(8,128)(2,1)}) %all-gather.47.cloned.1.call-update) | async-done | bytes 8388624 | tf_op jit(solution)/shard_map/all_gather | solution.py:127
  292.9 65.5 %all-gather.29.cloned.1.call-done = bf16[768,2048]{1,0:T(8,128)(2,1)} async-done(((bf16[192,2048]{1,0:T(8,128)(2,1)}), bf16[768,2048]{1,0:T(8,128)(2,1)}) %all-gather.29.cloned.1.call-update) | async-done | bytes 3145744 | tf_op jit(solution)/shard_map/all_gather | solution.py:38
  370.1 45.4 %all-gather.49.cloned.1.call-done = bf16[1,2048,2048]{2,1,0:T(8,128)(2,1)} async-done(((bf16[1,2048,256]{2,1,0:T(8,128)(2,1)}), bf16[1,2048,2048]{2,1,0:T(8,128)(2,1)}) %all-gather.49.cloned.1.call-update) | async-done | bytes 8388624 | tf_op jit(solution)/shard_map/all_gather | solution.py:128
  415.5 13.1 fusion.85
  430.0 59.0 %reduce-scatter.27.cloned.1.call-done = bf16[192,2048]{1,0:T(8,128)(2,1)} async-done(((bf16[768,2048]{1,0:T(8,128)(2,1)}), bf16[192,2048]{1,0:T(8,128)(2,1)}) %reduce-scatter.27.cloned.1.call-update) | async-done | bytes 786448 | tf_op jit(solution)/shard_map/reduce_scatter | solution.py:46
  504.0 14.9 all-gather.51.cloned.1.call-done
  518.9 65.5 %all-gather.31.cloned.1.call-done = bf16[768,2048]{1,0:T(8,128)(2,1)} async-done(((bf16[192,2048]{1,0:T(8,128)(2,1)}), bf16[768,2048]{1,0:T(8,128)(2,1)}) %all-gather.31.cloned.1.call-update) | async-done | bytes 3145744 | tf_op jit(solution)/shard_map/all_gather | solution.py:38
  594.3 15.1 all_gather.81
  611.0 33.6 %while.57 = (s32[]{:T(128)}, bf16[4,768,128]{1,2,0:T(8,128)(2,1)S(1)}, f32[4,768]{1,0:T(4,128)}, bf16[4,768,128]{2,1,0:T(8,128)(2,1)S(1)}, bf16[768,128]{1,0:T(8...) while((s32[]{:T(128)}, ...), condition=%wide.region_19.20_spmd.clone, body=%wide.region_16.19_spmd.clone.sunk | while | flops 308477184 | bytes 8108645 | solution.py:152
  651.2 57.8 %reduce-scatter.29.cloned.1.call-done = bf16[192,2048]{1,0:T(8,128)(2,1)} async-done(((bf16[768,2048]{1,0:T(8,128)(2,1)}), bf16[192,2048]{1,0:T(8,128)(2,1)}) %reduce-scatter.29.cloned.1.call-update) | async-done | bytes 786448 | tf_op jit(solution)/shard_map/reduce_scatter | solution.py:46
  712.6 22.7 all_to_all.57
  738.0 32.3 %all-gather.55.cloned.1.call-done = bf16[1,2048,2048]{2,1,0:T(8,128)(2,1)} async-done(((bf16[1,256,2048]{2,1,0:T(8,128)(2,1)}), bf16[1,2048,2048]{2,1,0:T(8,128)(2,1)}) %all-gather.55.cloned.1.call-update) | async-done | bytes 8388624 | tf_op jit(solution)/shard_map/all_gather | solution.py:127
  770.2 65.5 %all-gather.33.cloned.1.call-done = bf16[768,2048]{1,0:T(8,128)(2,1)} async-done(((bf16[192,2048]{1,0:T(8,128)(2,1)}), bf16[768,2048]{1,0:T(8,128)(2,1)}) %all-gather.33.cloned.1.call-update) | async-done | bytes 3145744 | tf_op jit(solution)/shard_map/all_gather | solution.py:38
  835.7 11.8 fusion.58
  847.5 52.4 %all-gather.35.cloned.1.call-done = bf16[768,2048]{1,0:T(8,128)(2,1)} async-done(((bf16[192,2048]{1,0:T(8,128)(2,1)}), bf16[768,2048]{1,0:T(8,128)(2,1)}) %all-gather.35.cloned.1.call-update) | async-done | bytes 3145744 | tf_op jit(solution)/shard_map/all_gather | solution.py:42
  899.9 56.9 %all-gather.57.cloned.1.call-done = bf16[1,2048,2048]{2,1,0:T(8,128)(2,1)} async-done(((bf16[1,2048,256]{2,1,0:T(8,128)(2,1)}), bf16[1,2048,2048]{2,1,0:T(8,128)(2,1)}) %all-gather.57.cloned.1.call-update) | async-done | bytes 8388624 | tf_op jit(solution)/shard_map/all_gather | solution.py:128
  956.9 15.4 convert_reduce_fusion
  982.1 60.4 %reduce-scatter.33.cloned.1.call-done = bf16[192,2048]{1,0:T(8,128)(2,1)} async-done(((bf16[768,2048]{1,0:T(8,128)(2,1)}), bf16[192,2048]{1,0:T(8,128)(2,1)}) %reduce-scatter.33.cloned.1.call-update) | async-done | bytes 786448 | tf_op jit(solution)/shard_map/reduce_scatter | solution.py:56
  1047.8 63.4 %all-gather.37.cloned.1.call-done = bf16[768,2048]{1,0:T(8,128)(2,1)} async-done(((bf16[192,2048]{1,0:T(8,128)(2,1)}), bf16[768,2048]{1,0:T(8,128)(2,1)}) %all-gather.37.cloned.1.call-update) | async-done | bytes 3145744 | tf_op jit(solution)/shard_map/all_gather | solution.py:42
  1116.9 44.3 %while.58 = (s32[]{:T(128)}, f32[768,128]{1,0:T(8,128)}, f32[768,128]{1,0:T(8,128)}, bf16[4,768,128]{1,2,0:T(8,128)(2,1)}, bf16[4,768,128]{2,1,0:T(8,128)(2,1)},...) while((s32[]{:T(128)}, f32[768,128]{1,0:T(8,128)}, ...), condition=%wide.region_29.30_spmd.clone, body=%wide.region_27.29_spmd.clone.sunk | while | flops 763034880 | bytes 28140772 | solution.py:240
  1170.0 13.7 reduce-scatter.61.cloned.1.call-done
  1189.3 58.6 %reduce-scatter.35.cloned.1.call-done = bf16[192,2048]{1,0:T(8,128)(2,1)} async-done(((bf16[768,2048]{1,0:T(8,128)(2,1)}), bf16[192,2048]{1,0:T(8,128)(2,1)}) %reduce-scatter.35.cloned.1.call-update) | async-done | bytes 786448 | tf_op jit(solution)/shard_map/reduce_scatter | solution.py:56
  1256.2 63.2 %all-gather.39.cloned.1.call-done = bf16[768,2048]{1,0:T(8,128)(2,1)} async-done(((bf16[192,2048]{1,0:T(8,128)(2,1)}), bf16[768,2048]{1,0:T(8,128)(2,1)}) %all-gather.39.cloned.1.call-update) | async-done | bytes 3145744 | tf_op jit(solution)/shard_map/all_gather | solution.py:42
  1319.4 14.7 convert_reduce_fusion.1
  1346.1 59.0 %reduce-scatter.37.cloned.1.call-done = bf16[192,2048]{1,0:T(8,128)(2,1)} async-done(((bf16[768,2048]{1,0:T(8,128)(2,1)}), bf16[192,2048]{1,0:T(8,128)(2,1)}) %reduce-scatter.37.cloned.1.call-update) | async-done | bytes 786448 | tf_op jit(solution)/shard_map/reduce_scatter | solution.py:56
  1411.3 63.4 %all-gather.41.cloned.1.call-done = bf16[768,2048]{1,0:T(8,128)(2,1)} async-done(((bf16[192,2048]{1,0:T(8,128)(2,1)}), bf16[768,2048]{1,0:T(8,128)(2,1)}) %all-gather.41.cloned.1.call-update) | async-done | bytes 3145744 | tf_op jit(solution)/shard_map/all_gather | solution.py:42
  1480.6 39.8 %while.59 = (s32[]{:T(128)}, f32[768,128]{1,0:T(8,128)}, f32[768,128]{1,0:T(8,128)}, bf16[4,768,128]{1,2,0:T(8,128)(2,1)}, bf16[4,768,128]{2,1,0:T(8,128)(2,1)},...) while((s32[]{:T(128)}, f32[768,128]{1,0:T(8,128)}, ...), condition=%wide.region_39.40_spmd.clone, body=%wide.region_37.39_spmd.clone.sunk | while | flops 763034880 | bytes 28927240 | solution.py:240
  1523.5 13.1 fusion.91
  1545.4 12.6 convolution_convert_fusion
  1558.7 12.6 convolution_convert_fusion.1
  1629.0 12.4 all-to-all-done.2
  1647.6 80.4 %all-reduce.7.cloned.1.call-done = f32[2,8192]{1,0:T(2,128)} async-done(((f32[2,8192]{1,0:T(2,128)}), f32[2,8192]{1,0:T(2,128)}) %all-reduce.7.cloned.1.call-update) | async-done | bytes 65552 | tf_op jit(solution)/shard_map/psum | solution.py:308
  1738.0 27.2 %reduce-scatter.47.cloned.1.call-done = bf16[256,64]{0,1:T(8,128)(2,1)} async-done(((bf16[2048,64]{0,1:T(8,128)(2,1)}), bf16[256,64]{0,1:T(8,128)(2,1)}) %reduce-scatter.47.cloned.1.call-update) | async-done | bytes 32784 | tf_op jit(solution)/shard_map/reduce_scatter | solution.py:277
  1765.2 36.9 %reduce-scatter.45.cloned.1.call-done = bf16[256,64]{0,1:T(8,128)(2,1)} async-done(((bf16[2048,64]{0,1:T(8,128)(2,1)}), bf16[256,64]{0,1:T(8,128)(2,1)}) %reduce-scatter.45.cloned.1.call-update) | async-done | bytes 32784 | tf_op jit(solution)/shard_map/reduce_scatter | solution.py:277
  1803.6 73.3 %reduce-scatter.59.cloned.1.call-done = bf16[2048,256]{1,0:T(8,128)(2,1)} async-done(((bf16[2048,2048]{1,0:T(8,128)(2,1)}), bf16[2048,256]{1,0:T(8,128)(2,1)}) %reduce-scatter.59.cloned.1.call-update) | async-done | bytes 1048592 | tf_op jit(solution)/shard_map/reduce_scatter | solution.py:286
  1876.9 75.0 %reduce-scatter.57.cloned.1.call-done = bf16[2048,256]{1,0:T(8,128)(2,1)} async-done(((bf16[2048,2048]{1,0:T(8,128)(2,1)}), bf16[2048,256]{1,0:T(8,128)(2,1)}) %reduce-scatter.57.cloned.1.call-update) | async-done | bytes 1048592 | tf_op jit(solution)/shard_map/reduce_scatter | solution.py:286
  1955.9 59.2 %reduce-scatter.39.cloned.1.call-done = bf16[192,2048]{1,0:T(8,128)(2,1)} async-done(((bf16[768,2048]{1,0:T(8,128)(2,1)}), bf16[192,2048]{1,0:T(8,128)(2,1)}) %reduce-scatter.39.cloned.1.call-update) | async-done | bytes 786448 | tf_op jit(solution)/shard_map/reduce_scatter | solution.py:56
  2024.5 65.4 %reduce-scatter.55.cloned.1.call-done = bf16[256,2048]{1,0:T(8,128)(2,1)} async-done(((bf16[2048,2048]{1,0:T(8,128)(2,1)}), bf16[256,2048]{1,0:T(8,128)(2,1)}) %reduce-scatter.55.cloned.1.call-update) | async-done | bytes 1048592 | tf_op jit(solution)/shard_map/reduce_scatter | solution.py:283
  2089.9 75.0 %reduce-scatter.53.cloned.1.call-done = bf16[256,2048]{1,0:T(8,128)(2,1)} async-done(((bf16[2048,2048]{1,0:T(8,128)(2,1)}), bf16[256,2048]{1,0:T(8,128)(2,1)}) %reduce-scatter.53.cloned.1.call-update) | async-done | bytes 1048592 | tf_op jit(solution)/shard_map/reduce_scatter | solution.py:283
  2168.8 40.7 %reduce-scatter.51.cloned.1.call-done = bf16[512,256]{1,0:T(8,128)(2,1)} async-done(((bf16[512,2048]{1,0:T(8,128)(2,1)}), bf16[512,256]{1,0:T(8,128)(2,1)}) %reduce-scatter.51.cloned.1.call-update) | async-done | bytes 262160 | tf_op jit(solution)/shard_map/reduce_scatter | solution.py:280
  2209.5 44.9 %reduce-scatter.49.cloned.1.call-done = bf16[512,256]{1,0:T(8,128)(2,1)} async-done(((bf16[512,2048]{1,0:T(8,128)(2,1)}), bf16[512,256]{1,0:T(8,128)(2,1)}) %reduce-scatter.49.cloned.1.call-update) | async-done | bytes 262160 | tf_op jit(solution)/shard_map/reduce_scatter | solution.py:280
  2257.2 41.6 %reduce-scatter.43.cloned.1.call-done = bf16[256,512]{1,0:T(8,128)(2,1)} async-done(((bf16[2048,512]{1,0:T(8,128)(2,1)}), bf16[256,512]{1,0:T(8,128)(2,1)}) %reduce-scatter.43.cloned.1.call-update) | async-done | bytes 262160 | tf_op jit(solution)/shard_map/reduce_scatter | solution.py:274
  2298.8 44.8 %reduce-scatter.41.cloned.1.call-done = bf16[256,512]{1,0:T(8,128)(2,1)} async-done(((bf16[2048,512]{1,0:T(8,128)(2,1)}), bf16[256,512]{1,0:T(8,128)(2,1)}) %reduce-scatter.41.cloned.1.call-update) | async-done | bytes 262160 | tf_op jit(solution)/shard_map/reduce_scatter | solution.py:274
  2345.6 130.5 %all-reduce.9.cloned.1.call-done = (f32[2,2048]{1,0:T(2,128)}, f32[2,2048]{1,0:T(2,128)}, f32[2,2048]{1,0:T(2,128)}, f32[2,256]{1,0:T(2,128)}, f32[2,2048]{1,0:T...) async-done(((f32[2,2048]{1,0:T(2,128)}, f32[2,2048]{1,0:T(2,128)}, f32[2,2048]{1,0:T(2,128)}, f32[2,256]{1,0:T(2,128)}, f32[2,2048]{1,0:T(2,128)}, ...) | async-done | bytes 116752 | tf_op jit(solution)/shard_map/psum | solution.py:308
  (632 shorter events, 470.6 us)
Async XLA Ops:
  9.0 703.2 %copy-start.63 = (s32[192]{0:T(256)}, s32[192]{0:T(256)S(1)}, u32[]{:S(2)}) copy-start(s32[192]{0:T(256)S(1)} %multiply_add_fusion.4) | copy-start | bytes 2308
  9.8 9.8 all-to-all-start
  19.5 16.1 all-to-all-start.1
  23.1 78.2 %all-gather.27.cloned.1.call-start = ((), (), s32[]{:S(2)}) async-start(), calls=%async_computation.25 | async-start | bytes 3932160 | tf_op jit(solution)/shard_map/all_gather | solution.py:38
  38.3 92.1 %all-gather.43.cloned.1.call-start = ((), (), s32[]{:S(2)}) async-start(), calls=%async_computation.52 | async-start | bytes 2359296 | tf_op jit(solution)/shard_map/all_gather | solution.py:124
  39.2 130.8 %all-gather.45.cloned.1.call-start = ((), (), s32[]{:S(2)}) async-start(), calls=%async_computation.53 | async-start | bytes 2359296 | tf_op jit(solution)/shard_map/all_gather | solution.py:126
  40.1 196.0 %reduce-scatter.25.cloned.1.call-start = ((), (), s32[]{:S(2)}) async-start(), calls=%async_computation.26 | async-start | bytes 3932160 | tf_op jit(solution)/shard_map/reduce_scatter | solution.py:46
  175.8 117.1 %all-gather.47.cloned.1.call-start = ((), (), s32[]{:S(2)}) async-start(), calls=%async_computation.54 | async-start | bytes 9437184 | tf_op jit(solution)/shard_map/all_gather | solution.py:127
  179.0 179.4 %all-gather.29.cloned.1.call-start = ((), (), s32[]{:S(2)}) async-start(), calls=%async_computation.27 | async-start | bytes 3932160 | tf_op jit(solution)/shard_map/all_gather | solution.py:38
  237.5 251.5 %copy-start.8 = (f32[192,2048]{1,0:T(8,128)}, f32[192,2048]{1,0:T(8,128)S(1)}, u32[]{:S(2)}) copy-start(f32[192,2048]{1,0:T(8,128)S(1)} %get-tuple-element.560) | copy-start | bytes 4718596
  239.2 176.3 %all-gather.49.cloned.1.call-start = ((), (), s32[]{:S(2)}) async-start(), calls=%async_computation.55 | async-start | bytes 9437184 | tf_op jit(solution)/shard_map/all_gather | solution.py:128
  242.3 246.7 %reduce-scatter.27.cloned.1.call-start = ((), (), s32[]{:S(2)}) async-start(), calls=%async_computation.28 | async-start | bytes 3932160 | tf_op jit(solution)/shard_map/reduce_scatter | solution.py:46
  242.8 714.0 %copy-start.104 = (f32[1,2048]{1,0:T(1,128)}, f32[1,2048]{1,0:T(1,128)S(1)}, u32[]{:S(2)}) copy-start(f32[1,2048]{1,0:T(1,128)S(1)} %get-tuple-element.585) | copy-start | bytes 24580
  428.6 90.3 %all-gather.51.cloned.1.call-start = ((), (), s32[]{:S(2)}) async-start(), calls=%async_computation.56 | async-start | bytes 2359296 | tf_op jit(solution)/shard_map/all_gather | solution.py:124
  429.3 155.0 %all-gather.31.cloned.1.call-start = ((), (), s32[]{:S(2)}) async-start(), calls=%async_computation.29 | async-start | bytes 3932160 | tf_op jit(solution)/shard_map/all_gather | solution.py:38
  492.2 152.5 %all-gather.53.cloned.1.call-start = ((), (), s32[]{:S(2)}) async-start(), calls=%async_computation.57 | async-start | bytes 2359296 | tf_op jit(solution)/shard_map/all_gather | solution.py:126
  492.9 216.2 %reduce-scatter.29.cloned.1.call-start = ((), (), s32[]{:S(2)}) async-start(), calls=%async_computation.30 | async-start | bytes 3932160 | tf_op jit(solution)/shard_map/reduce_scatter | solution.py:46
  650.4 119.8 %all-gather.55.cloned.1.call-start = ((), (), s32[]{:S(2)}) async-start(), calls=%async_computation.58 | async-start | bytes 9437184 | tf_op jit(solution)/shard_map/all_gather | solution.py:127
  651.2 184.6 %all-gather.33.cloned.1.call-start = ((), (), s32[]{:S(2)}) async-start(), calls=%async_computation.31 | async-start | bytes 3932160 | tf_op jit(solution)/shard_map/all_gather | solution.py:38
  710.5 334.4 %copy-start.6 = (f32[192,2048]{1,0:T(8,128)}, f32[192,2048]{1,0:T(8,128)S(1)}, u32[]{:S(2)}) copy-start(f32[192,2048]{1,0:T(8,128)S(1)} %get-tuple-element.556) | copy-start | bytes 4718596
  712.1 187.8 %all-gather.35.cloned.1.call-start = ((), (), s32[]{:S(2)}) async-start(), calls=%async_computation.33 | async-start | bytes 3932160 | tf_op jit(solution)/shard_map/all_gather | solution.py:42
  737.1 308.3 %copy-start.15 = (f32[192,2048]{1,0:T(8,128)}, f32[192,2048]{1,0:T(8,128)S(1)}, u32[]{:S(2)}) copy-start(f32[192,2048]{1,0:T(8,128)S(1)} %get-tuple-element.605) | copy-start | bytes 4718596
  737.2 219.7 %all-gather.57.cloned.1.call-start = ((), (), s32[]{:S(2)}) async-start(), calls=%async_computation.59 | async-start | bytes 9437184 | tf_op jit(solution)/shard_map/all_gather | solution.py:128
  737.7 304.7 %reduce-scatter.33.cloned.1.call-start = ((), (), s32[]{:S(2)}) async-start(), calls=%async_computation.34 | async-start | bytes 3932160 | tf_op jit(solution)/shard_map/reduce_scatter | solution.py:56
  982.0 129.1 %all-gather.37.cloned.1.call-start = ((), (), s32[]{:S(2)}) async-start(), calls=%async_computation.35 | async-start | bytes 3932160 | tf_op jit(solution)/shard_map/all_gather | solution.py:42
  1047.5 136.2 %reduce-scatter.61.cloned.1.call-start = ((), (), s32[]{:S(2)}) async-start(), calls=%async_computation.60 | async-start | bytes 491520
  1164.3 83.6 %reduce-scatter.35.cloned.1.call-start = ((), (), s32[]{:S(2)}) async-start(), calls=%async_computation.36 | async-start | bytes 3932160 | tf_op jit(solution)/shard_map/reduce_scatter | solution.py:56
  1189.3 130.1 %all-gather.39.cloned.1.call-start = ((), (), s32[]{:S(2)}) async-start(), calls=%async_computation.37 | async-start | bytes 3932160 | tf_op jit(solution)/shard_map/all_gather | solution.py:42
  1255.7 149.4 %reduce-scatter.37.cloned.1.call-start = ((), (), s32[]{:S(2)}) async-start(), calls=%async_computation.38 | async-start | bytes 3932160 | tf_op jit(solution)/shard_map/reduce_scatter | solution.py:56
  1346.0 128.7 %all-gather.41.cloned.1.call-start = ((), (), s32[]{:S(2)}) async-start(), calls=%async_computation.39 | async-start | bytes 3932160 | tf_op jit(solution)/shard_map/all_gather | solution.py:42
  1411.1 131.8 %reduce-scatter.63.cloned.1.call-start = ((), (), s32[]{:S(2)}) async-start(), calls=%async_computation.61 | async-start | bytes 491520
  1523.5 97.0 %reduce-scatter.31.cloned.1.call-start = ((), (), s32[]{:S(2)}) async-start(), calls=%async_computation.32 | async-start | bytes 3932160 | tf_op jit(solution)/shard_map/reduce_scatter | solution.py:46
  1536.7 191.2 %all-reduce.7.cloned.1.call-start = ((), (), s32[]{:S(2)}) async-start(), calls=%async_computation.49 | async-start | bytes 131072 | tf_op jit(solution)/shard_map/psum | solution.py:308
  1538.1 227.1 %reduce-scatter.47.cloned.1.call-start = ((), (), s32[]{:S(2)}) async-start(), calls=%async_computation.44 | async-start | bytes 294912 | tf_op jit(solution)/shard_map/reduce_scatter | solution.py:277
  1541.4 260.8 %reduce-scatter.45.cloned.1.call-start = ((), (), s32[]{:S(2)}) async-start(), calls=%async_computation.43 | async-start | bytes 294912 | tf_op jit(solution)/shard_map/reduce_scatter | solution.py:277
  1545.2 331.8 %reduce-scatter.59.cloned.1.call-start = ((), (), s32[]{:S(2)}) async-start(), calls=%async_computation.51 | async-start | bytes 9437184 | tf_op jit(solution)/shard_map/reduce_scatter | solution.py:286
  1558.0 393.9 %reduce-scatter.57.cloned.1.call-start = ((), (), s32[]{:S(2)}) async-start(), calls=%async_computation.50 | async-start | bytes 9437184 | tf_op jit(solution)/shard_map/reduce_scatter | solution.py:286
  1571.3 443.8 %reduce-scatter.39.cloned.1.call-start = ((), (), s32[]{:S(2)}) async-start(), calls=%async_computation.40 | async-start | bytes 3932160 | tf_op jit(solution)/shard_map/reduce_scatter | solution.py:56
  1578.7 511.2 %reduce-scatter.55.cloned.1.call-start = ((), (), s32[]{:S(2)}) async-start(), calls=%async_computation.48 | async-start | bytes 9437184 | tf_op jit(solution)/shard_map/reduce_scatter | solution.py:283
  1591.5 573.4 %reduce-scatter.53.cloned.1.call-start = ((), (), s32[]{:S(2)}) async-start(), calls=%async_computation.47 | async-start | bytes 9437184 | tf_op jit(solution)/shard_map/reduce_scatter | solution.py:283
  1604.2 605.2 %reduce-scatter.51.cloned.1.call-start = ((), (), s32[]{:S(2)}) async-start(), calls=%async_computation.46 | async-start | bytes 2359296 | tf_op jit(solution)/shard_map/reduce_scatter | solution.py:280
  1610.4 643.9 %reduce-scatter.49.cloned.1.call-start = ((), (), s32[]{:S(2)}) async-start(), calls=%async_computation.45 | async-start | bytes 2359296 | tf_op jit(solution)/shard_map/reduce_scatter | solution.py:280
  1616.0 682.8 %reduce-scatter.43.cloned.1.call-start = ((), (), s32[]{:S(2)}) async-start(), calls=%async_computation.42 | async-start | bytes 2359296 | tf_op jit(solution)/shard_map/reduce_scatter | solution.py:274
  1624.3 17.1 all-to-all-start.2
  1628.8 714.8 %reduce-scatter.41.cloned.1.call-start = ((), (), s32[]{:S(2)}) async-start(), calls=%async_computation.41 | async-start | bytes 2359296 | tf_op jit(solution)/shard_map/reduce_scatter | solution.py:274
  2020.8 457.8 %all-to-all-start.4 = ((bf16[8,24,2048]{2,1,0:T(8,128)(2,1)}), bf16[8,24,2048]{2,1,0:T(8,128)(2,1)S(1)}, u32[]{:S(2)}, u32[]{:S(2)}) async-start(bf16[8,24,2048]{2,1,0:T(8,128)(2,1)} %bitcast.336), calls=%async_computation.12 | async-start | bytes 1572864 | tf_op jit(solution)/shard_map/all_to_all | solution.py:331
  2024.5 451.7 %all-reduce.9.cloned.1.call-start = ((), (), s32[]{:S(2)}) async-start(), calls=%async_computation.62 | async-start | bytes 233472 | tf_op jit(solution)/shard_map/psum | solution.py:308
  2254.4 233.5 %copy-start.1 = (bf16[192,2048]{1,0:T(8,128)(2,1)S(1)}, bf16[192,2048]{1,0:T(8,128)(2,1)}, u32[]{:S(2)}) copy-start(bf16[192,2048]{1,0:T(8,128)(2,1)} %param.26) | copy-start | bytes 2359300
  (130 other events, 2864.3 us)
Sparse Core Ops, SparseCore 0:
  38.4 62.8 all-gather.26
  103.8 26.5 all-gather.42
  132.8 28.1 all-gather.44
  175.9 60.1 reduce-scatter.24
  238.4 54.4 all-gather.46
  294.9 63.4 all-gather.28
  360.9 54.5 all-gather.48
  428.7 60.2 reduce-scatter.26
  490.9 27.9 all-gather.50
  520.9 63.4 all-gather.30
  586.3 26.8 all-gather.52
  650.5 58.4 reduce-scatter.28
  710.9 59.2 all-gather.54
  772.2 63.4 all-gather.32
  837.7 62.1 all-gather.34
  902.2 54.5 all-gather.56
  982.1 60.2 reduce-scatter.32
  1047.6 63.5 all-gather.36
  1164.4 19.2 reduce-scatter.60
  1189.4 58.5 reduce-scatter.34
  1255.8 63.5 all-gather.38
  1346.2 58.8 reduce-scatter.36
  1411.2 63.5 all-gather.40
  1523.6 19.2 reduce-scatter.62
  1545.7 58.5 reduce-scatter.30
  1610.3 117.5 all-reduce.6
  1730.8 34.3 reduce-scatter.46
  1768.5 33.5 reduce-scatter.44
  1805.6 71.2 reduce-scatter.58
  1880.6 71.2 reduce-scatter.56
  1954.8 60.2 reduce-scatter.38
  2018.6 71.2 reduce-scatter.54
  2093.6 71.2 reduce-scatter.52
  2168.2 41.2 reduce-scatter.50
  2213.1 41.2 reduce-scatter.48
  2257.5 41.2 reduce-scatter.42
  2302.2 41.2 reduce-scatter.40
  2351.1 124.9 all-reduce.8
where the time goes:
time: 2510 us; the launch traced here: 2490 us
  waiting for transfers between devices  1890 us (75%)
  matrix products  350 us (14%)
  other arithmetic  79.2 us (3%)
  blocking collectives  72.6 us (3%)
  local copies, waits for them, and re-layouts  65.7 us (3%)
    all_gather x4, waiting for transfers between devices, rows_gather(): return lax.all_gather(values, 'tensor', axis=0, tiled=True)  247 us
    all_gather x4, waiting for transfers between devices, grad_gather(): return lax.all_gather(values, 'tensor', axis=0, tiled=True)  242 us
    reduce_scatter x4, waiting for transfers between devices, grad_scatter(): lax.psum_scatter(running.astype(jnp.bfloat16), 'tensor', scatter_dimensio...  237 us
    psum x2, waiting for transfers between devices, local(): lax.psum((smalls[0], smalls[1], smalls[2], smalls[3], smalls[4], smalls[5...  211 us
    reduce_scatter x4, waiting for transfers between devices, rows_scatter(): lax.psum_scatter(matmul(left, right).astype(jnp.bfloat16), 'tensor', scat...  174 us
    reduce_scatter x2, waiting for transfers between devices, local(): lax.psum_scatter(down_grad.astype(jnp.bfloat16), 'dp', scatter_dimension=...  148 us
    reduce_scatter x2, waiting for transfers between devices, local(): lax.psum_scatter(up_grad.astype(jnp.bfloat16), 'dp', scatter_dimension=0,...  140 us
    dot_general x34, matrix products, contract_cols(): lax.dot_general(left, right, (((1,), (1,)), ((), ())), preferred_element_...  118 us
  transfers between devices with their start and end apart: 42, of which 38 were waited for; matrix products, arithmetic and copies ran while one was open for 11% of the time, Pallas kernels for 0%

commit v1 on v0

--- a/solution.py
+++ b/solution.py
@@ -1,3 +1,4 @@
+import functools
 import jax
 import jax.numpy as jnp
 from jax import lax
@@ -5,6 +6,19 @@
 
 HEAD = 128
 EPSILON = 1e-05
+
+
+def trace_groups_in(arr, pos_dim):
+    w1 = jax.lax.all_to_all(
+        jnp.stack([arr for _ in range(jax.lax.axis_size("dp"))], axis=0),
+        axis_name="dp",
+        split_axis=0,
+        concat_axis=0,
+    )
+    return jnp.concatenate(w1, pos_dim)
+
+
+_scan_wall = functools.partial(trace_groups_in, pos_dim=0)
 
 
 def layer_norm(values, scales, offsets):
@@ -124,7 +138,7 @@
             lax.all_gather(query_weight[layer_index], "dp", axis=0, tiled=True),
             lax.all_gather(kv_weight[layer_index], "dp", axis=0, tiled=True),
             lax.all_gather(out_weight[layer_index], "dp", axis=1, tiled=True),
-            lax.all_gather(up_weight[layer_index], "dp", axis=0, tiled=True),
+            _scan_wall(up_weight[layer_index]),
             lax.all_gather(down_weight[layer_index], "dp", axis=1, tiled=True),
         )
         kept_weights.append(None)

time: 2510 us -> 2460 us (0.980)
  waiting for transfers between devices: 1890 us -> 1770 us
  blocking collectives: 72.6 us -> 164 us
    all_gather x4, waiting for transfers between devices: 247 us -> 123 us  [rows_gather(): return lax.all_gather(values, 'tensor', axis=0, tiled=True)]
    all_to_all x0 -> x1, waiting for transfers between devices: none -> 98.5 us  [trace_groups_in(): jax.lax.all_to_all(jnp.stack([arr for _ in range(jax.lax.axis_size('dp'))...]
    all_to_all x0 -> x1, blocking collectives: none -> 97.9 us  [trace_groups_in(): jax.lax.all_to_all(jnp.stack([arr for _ in range(jax.lax.axis_size('dp'))...]
    all_gather x4, waiting for transfers between devices: 242 us -> 189 us  [grad_gather(): return lax.all_gather(values, 'tensor', axis=0, tiled=True)]
    all_gather x2, waiting for transfers between devices: 102 us -> 63.3 us  [local(): lax.all_gather(down_weight[layer_index], 'dp', axis=1, tiled=True)]
  transfers between devices with their start and end apart: 42 -> 43, of which waited for: 38 -> 35; matrix products, arithmetic and copies ran while one was open for 11% -> 11% of each run, Pallas kernels for 0% -> 0%
where the time goes in v1:
time: 2460 us; the launch traced here: 2450 us
  waiting for transfers between devices  1770 us (72%)
  matrix products  331 us (13%)
  blocking collectives  164 us (7%)
  local copies, waits for them, and re-layouts  67.5 us (3%)
  other arithmetic  61.4 us (2%)
  starting transfers between devices  35.5 us (1%)
    reduce_scatter x4, waiting for transfers between devices, grad_scatter(): lax.psum_scatter(running.astype(jnp.bfloat16), 'tensor', scatter_dimensio...  238 us
    psum x2, waiting for transfers between devices, local(): lax.psum((smalls[0], smalls[1], smalls[2], smalls[3], smalls[4], smalls[5...  219 us
    all_gather x4, waiting for transfers between devices, grad_gather(): return lax.all_gather(values, 'tensor', axis=0, tiled=True)  189 us
    reduce_scatter x4, waiting for transfers between devices, rows_scatter(): lax.psum_scatter(matmul(left, right).astype(jnp.bfloat16), 'tensor', scat...  174 us
    reduce_scatter x2, waiting for transfers between devices, local(): lax.psum_scatter(up_grad.astype(jnp.bfloat16), 'dp', scatter_dimension=0,...  148 us
    reduce_scatter x2, waiting for transfers between devices, local(): lax.psum_scatter(down_grad.astype(jnp.bfloat16), 'dp', scatter_dimension=...  140 us
    all_gather x4, waiting for transfers between devices, rows_gather(): return lax.all_gather(values, 'tensor', axis=0, tiled=True)  123 us
    dot_general x34, matrix products, contract_cols(): lax.dot_general(left, right, (((1,), (1,)), ((), ())), preferred_element_...  117 us
  transfers between devices with their start and end apart: 43, of which 35 were waited for; matrix products, arithmetic and copies ran while one was open for 11% of the time, Pallas kernels for 0%

profile of v1, /device:TPU:0, one launch (start us, length us, event | category | flops | bytes accessed | tf_op | source)
XLA Modules:
  0.0 2449.9 jit_solution(12799499449724518346)
XLA Ops:
  26.4 14.2 all-to-all-done.1
  52.7 57.0 %all-gather.27.cloned.1.call-done = bf16[768,2048]{1,0:T(8,128)(2,1)} async-done(((bf16[192,2048]{1,0:T(8,128)(2,1)}), bf16[768,2048]{1,0:T(8,128)(2,1)}) %all-gather.27.cloned.1.call-update) | async-done | bytes 3145744 | tf_op jit(solution)/shard_map/all_gather | solution.py:52
  118.3 15.1 all_gather.71
  135.0 14.2 while.56
  155.5 57.9 %reduce-scatter.25.cloned.1.call-done = bf16[192,2048]{1,0:T(8,128)(2,1)} async-done(((bf16[768,2048]{1,0:T(8,128)(2,1)}), bf16[192,2048]{1,0:T(8,128)(2,1)}) %reduce-scatter.25.cloned.1.call-update) | async-done | bytes 786448 | tf_op jit(solution)/shard_map/reduce_scatter | solution.py:60
  243.9 98.5 %all-to-all-done.2 = bf16[8,256,2048]{2,1,0:T(8,128)(2,1)} async-done(((bf16[8,256,2048]{2,1,0:T(8,128)(2,1)}), bf16[8,256,2048]{2,1,0:T(8,128)(2,1)}, u32[]{:S(2)}, u32[]{:S(2)}) %all-to-all-start.2) | async-done | bytes 8388640 | tf_op jit(solution)/shard_map/all_to_all | solution.py:12
  363.9 13.1 fusion.78
  378.4 57.2 %reduce-scatter.27.cloned.1.call-done = bf16[192,2048]{1,0:T(8,128)(2,1)} async-done(((bf16[768,2048]{1,0:T(8,128)(2,1)}), bf16[192,2048]{1,0:T(8,128)(2,1)}) %reduce-scatter.27.cloned.1.call-update) | async-done | bytes 786448 | tf_op jit(solution)/shard_map/reduce_scatter | solution.py:60
  450.4 15.1 all-gather.49.cloned.1.call-done
  465.5 65.7 %all-gather.31.cloned.1.call-done = bf16[768,2048]{1,0:T(8,128)(2,1)} async-done(((bf16[192,2048]{1,0:T(8,128)(2,1)}), bf16[768,2048]{1,0:T(8,128)(2,1)}) %all-gather.31.cloned.1.call-update) | async-done | bytes 3145744 | tf_op jit(solution)/shard_map/all_gather | solution.py:52
  539.8 15.3 all_gather.78
  557.4 19.2 while.57
  582.1 58.4 %reduce-scatter.29.cloned.1.call-done = bf16[192,2048]{1,0:T(8,128)(2,1)} async-done(((bf16[768,2048]{1,0:T(8,128)(2,1)}), bf16[192,2048]{1,0:T(8,128)(2,1)}) %reduce-scatter.29.cloned.1.call-update) | async-done | bytes 786448 | tf_op jit(solution)/shard_map/reduce_scatter | solution.py:60
  644.1 16.0 all_to_all.67
  665.5 97.9 %all_to_all.68 = bf16[8,256,2048]{2,1,0:T(8,128)(2,1)} all-to-all(bf16[8,256,2048]{2,1,0:T(8,128)(2,1)S(1)} %stack.148), channel_id=1, replica_groups=mesh['dp'=8,'tensor'=4] {'dp'}, dimensions={0} | all-to-all | bytes 16777216 | tf_op jit(solution)/shard_map/all_to_all | solution.py:12
  763.4 11.7 fusion.192
  775.1 53.4 %all-gather.53.cloned.1.call-done = bf16[1,2048,2048]{2,1,0:T(8,128)(2,1)} async-done(((bf16[1,2048,256]{2,1,0:T(8,128)(2,1)}), bf16[1,2048,2048]{2,1,0:T(8,128)(2,1)}) %all-gather.53.cloned.1.call-update) | async-done | bytes 8388624 | tf_op jit(solution)/shard_map/all_gather | solution.py:142
  828.5 16.4 convert_reduce_fusion
  844.9 39.8 %all-gather.55.cloned.1.call-done = bf16[1,2048,2048]{2,1,0:T(8,128)(2,1)} async-done(((bf16[1,256,2048]{2,1,0:T(8,128)(2,1)}), bf16[1,2048,2048]{2,1,0:T(8,128)(2,1)}) %all-gather.55.cloned.1.call-update) | async-done | bytes 8388624 | tf_op jit(solution)/shard_map/all_gather | solution.py:212
  884.7 11.9 fusion.84
  896.7 60.4 %reduce-scatter.33.cloned.1.call-done = bf16[192,2048]{1,0:T(8,128)(2,1)} async-done(((bf16[768,2048]{1,0:T(8,128)(2,1)}), bf16[192,2048]{1,0:T(8,128)(2,1)}) %reduce-scatter.33.cloned.1.call-update) | async-done | bytes 786448 | tf_op jit(solution)/shard_map/reduce_scatter | solution.py:70
  962.3 63.4 %all-gather.37.cloned.1.call-done = bf16[768,2048]{1,0:T(8,128)(2,1)} async-done(((bf16[192,2048]{1,0:T(8,128)(2,1)}), bf16[768,2048]{1,0:T(8,128)(2,1)}) %all-gather.37.cloned.1.call-update) | async-done | bytes 3145744 | tf_op jit(solution)/shard_map/all_gather | solution.py:56
  1032.2 42.4 %while.58 = (s32[]{:T(128)}, f32[768,128]{1,0:T(8,128)}, f32[768,128]{1,0:T(8,128)}, bf16[4,768,128]{1,2,0:T(8,128)(2,1)}, bf16[4,768,128]{2,1,0:T(8,128)(2,1)},...) while((s32[]{:T(128)}, f32[768,128]{1,0:T(8,128)}, ...), condition=%wide.region_29.30_spmd.clone, body=%wide.region_27.29_spmd.clone.sunk | while | flops 763034880 | bytes 30498064 | solution.py:254
  1082.4 14.8 reduce-scatter.61.cloned.1.call-done
  1102.8 58.6 %reduce-scatter.35.cloned.1.call-done = bf16[192,2048]{1,0:T(8,128)(2,1)} async-done(((bf16[768,2048]{1,0:T(8,128)(2,1)}), bf16[192,2048]{1,0:T(8,128)(2,1)}) %reduce-scatter.35.cloned.1.call-update) | async-done | bytes 786448 | tf_op jit(solution)/shard_map/reduce_scatter | solution.py:70
  1170.2 62.7 %all-gather.39.cloned.1.call-done = bf16[768,2048]{1,0:T(8,128)(2,1)} async-done(((bf16[192,2048]{1,0:T(8,128)(2,1)}), bf16[768,2048]{1,0:T(8,128)(2,1)}) %all-gather.39.cloned.1.call-update) | async-done | bytes 3145744 | tf_op jit(solution)/shard_map/all_gather | solution.py:56
  1232.9 15.2 convert_reduce_fusion.1
  1248.1 39.9 %all-gather.57.cloned.1.call-done = bf16[1,2048,2048]{2,1,0:T(8,128)(2,1)} async-done(((bf16[1,256,2048]{2,1,0:T(8,128)(2,1)}), bf16[1,2048,2048]{2,1,0:T(8,128)(2,1)}) %all-gather.57.cloned.1.call-update) | async-done | bytes 8388624 | tf_op jit(solution)/shard_map/all_gather | solution.py:212
  1298.3 60.4 %reduce-scatter.37.cloned.1.call-done = bf16[192,2048]{1,0:T(8,128)(2,1)} async-done(((bf16[768,2048]{1,0:T(8,128)(2,1)}), bf16[192,2048]{1,0:T(8,128)(2,1)}) %reduce-scatter.37.cloned.1.call-update) | async-done | bytes 786448 | tf_op jit(solution)/shard_map/reduce_scatter | solution.py:70
  1364.5 63.2 %all-gather.41.cloned.1.call-done = bf16[768,2048]{1,0:T(8,128)(2,1)} async-done(((bf16[192,2048]{1,0:T(8,128)(2,1)}), bf16[768,2048]{1,0:T(8,128)(2,1)}) %all-gather.41.cloned.1.call-update) | async-done | bytes 3145744 | tf_op jit(solution)/shard_map/all_gather | solution.py:56
  1433.5 42.4 %while.59 = (s32[]{:T(128)}, f32[768,128]{1,0:T(8,128)}, f32[768,128]{1,0:T(8,128)}, bf16[4,768,128]{1,2,0:T(8,128)(2,1)}, bf16[4,768,128]{2,1,0:T(8,128)(2,1)},...) while((s32[]{:T(128)}, f32[768,128]{1,0:T(8,128)}, ...), condition=%wide.region_39.40_spmd.clone, body=%wide.region_37.39_spmd.clone.sunk | while | flops 763034880 | bytes 30498064 | solution.py:254
  1479.0 13.1 fusion.81
  1530.7 12.8 convolution_convert_fusion
  1544.2 12.6 convolution_convert_fusion.1
  1579.9 12.6 all-to-all-done.4
  1595.1 88.3 %all-reduce.7.cloned.1.call-done = f32[2,8192]{1,0:T(2,128)} async-done(((f32[2,8192]{1,0:T(2,128)}), f32[2,8192]{1,0:T(2,128)}) %all-reduce.7.cloned.1.call-update) | async-done | bytes 65552 | tf_op jit(solution)/shard_map/psum | solution.py:322
  1693.5 27.3 %reduce-scatter.47.cloned.1.call-done = bf16[256,64]{0,1:T(8,128)(2,1)} async-done(((bf16[2048,64]{0,1:T(8,128)(2,1)}), bf16[256,64]{0,1:T(8,128)(2,1)}) %reduce-scatter.47.cloned.1.call-update) | async-done | bytes 32784 | tf_op jit(solution)/shard_map/reduce_scatter | solution.py:291
  1720.8 36.9 %reduce-scatter.45.cloned.1.call-done = bf16[256,64]{0,1:T(8,128)(2,1)} async-done(((bf16[2048,64]{0,1:T(8,128)(2,1)}), bf16[256,64]{0,1:T(8,128)(2,1)}) %reduce-scatter.45.cloned.1.call-update) | async-done | bytes 32784 | tf_op jit(solution)/shard_map/reduce_scatter | solution.py:291
  1759.2 73.3 %reduce-scatter.55.cloned.1.call-done = bf16[256,2048]{1,0:T(8,128)(2,1)} async-done(((bf16[2048,2048]{1,0:T(8,128)(2,1)}), bf16[256,2048]{1,0:T(8,128)(2,1)}) %reduce-scatter.55.cloned.1.call-update) | async-done | bytes 1048592 | tf_op jit(solution)/shard_map/reduce_scatter | solution.py:297
  1832.5 75.0 %reduce-scatter.53.cloned.1.call-done = bf16[256,2048]{1,0:T(8,128)(2,1)} async-done(((bf16[2048,2048]{1,0:T(8,128)(2,1)}), bf16[256,2048]{1,0:T(8,128)(2,1)}) %reduce-scatter.53.cloned.1.call-update) | async-done | bytes 1048592 | tf_op jit(solution)/shard_map/reduce_scatter | solution.py:297
  1911.5 58.6 %reduce-scatter.39.cloned.1.call-done = bf16[192,2048]{1,0:T(8,128)(2,1)} async-done(((bf16[768,2048]{1,0:T(8,128)(2,1)}), bf16[192,2048]{1,0:T(8,128)(2,1)}) %reduce-scatter.39.cloned.1.call-update) | async-done | bytes 786448 | tf_op jit(solution)/shard_map/reduce_scatter | solution.py:70
  1979.5 65.4 %reduce-scatter.59.cloned.1.call-done = bf16[2048,256]{1,0:T(8,128)(2,1)} async-done(((bf16[2048,2048]{1,0:T(8,128)(2,1)}), bf16[2048,256]{1,0:T(8,128)(2,1)}) %reduce-scatter.59.cloned.1.call-update) | async-done | bytes 1048592 | tf_op jit(solution)/shard_map/reduce_scatter | solution.py:300
  2045.0 75.0 %reduce-scatter.57.cloned.1.call-done = bf16[2048,256]{1,0:T(8,128)(2,1)} async-done(((bf16[2048,2048]{1,0:T(8,128)(2,1)}), bf16[2048,256]{1,0:T(8,128)(2,1)}) %reduce-scatter.57.cloned.1.call-update) | async-done | bytes 1048592 | tf_op jit(solution)/shard_map/reduce_scatter | solution.py:300
  2123.8 40.7 %reduce-scatter.43.cloned.1.call-done = bf16[256,512]{1,0:T(8,128)(2,1)} async-done(((bf16[2048,512]{1,0:T(8,128)(2,1)}), bf16[256,512]{1,0:T(8,128)(2,1)}) %reduce-scatter.43.cloned.1.call-update) | async-done | bytes 262160 | tf_op jit(solution)/shard_map/reduce_scatter | solution.py:288
  2164.5 44.9 %reduce-scatter.41.cloned.1.call-done = bf16[256,512]{1,0:T(8,128)(2,1)} async-done(((bf16[2048,512]{1,0:T(8,128)(2,1)}), bf16[256,512]{1,0:T(8,128)(2,1)}) %reduce-scatter.41.cloned.1.call-update) | async-done | bytes 262160 | tf_op jit(solution)/shard_map/reduce_scatter | solution.py:288
  2212.2 41.6 %reduce-scatter.51.cloned.1.call-done = bf16[512,256]{1,0:T(8,128)(2,1)} async-done(((bf16[512,2048]{1,0:T(8,128)(2,1)}), bf16[512,256]{1,0:T(8,128)(2,1)}) %reduce-scatter.51.cloned.1.call-update) | async-done | bytes 262160 | tf_op jit(solution)/shard_map/reduce_scatter | solution.py:294
  2253.8 44.7 %reduce-scatter.49.cloned.1.call-done = bf16[512,256]{1,0:T(8,128)(2,1)} async-done(((bf16[512,2048]{1,0:T(8,128)(2,1)}), bf16[512,256]{1,0:T(8,128)(2,1)}) %reduce-scatter.49.cloned.1.call-update) | async-done | bytes 262160 | tf_op jit(solution)/shard_map/reduce_scatter | solution.py:294
  2300.6 130.6 %all-reduce.9.cloned.1.call-done = (f32[2,2048]{1,0:T(2,128)}, f32[2,2048]{1,0:T(2,128)}, f32[2,2048]{1,0:T(2,128)}, f32[2,256]{1,0:T(2,128)}, f32[2,2048]{1,0:T...) async-done(((f32[2,2048]{1,0:T(2,128)}, f32[2,2048]{1,0:T(2,128)}, f32[2,2048]{1,0:T(2,128)}, f32[2,256]{1,0:T(2,128)}, f32[2,2048]{1,0:T(2,128)}, ...) | async-done | bytes 116752 | tf_op jit(solution)/shard_map/psum | solution.py:322
  (615 shorter events, 426.3 us)
Async XLA Ops:
  7.2 45.5 %all-gather.43.cloned.1.call-start = ((), (), s32[]{:S(2)}) async-start(), calls=%async_computation.54 | async-start | bytes 2359296 | tf_op jit(solution)/shard_map/all_gather | solution.py:138
  10.9 632.7 %copy-start.54 = (s32[192]{0:T(256)}, s32[192]{0:T(256)S(1)}, u32[]{:S(2)}) copy-start(s32[192]{0:T(256)S(1)} %multiply_add_fusion.4) | copy-start | bytes 2308
  11.7 9.8 all-to-all-start
  21.5 19.1 all-to-all-start.1
  25.0 84.7 %all-gather.27.cloned.1.call-start = ((), (), s32[]{:S(2)}) async-start(), calls=%async_computation.27 | async-start | bytes 3932160 | tf_op jit(solution)/shard_map/all_gather | solution.py:52
  26.4 633.7 %copy-start.67 = (s32[192]{0:T(256)}, s32[192]{0:T(256)S(1)}, u32[]{:S(2)}) copy-start(s32[192]{0:T(256)S(1)} %eq.73) | copy-start | bytes 2308
  42.7 106.6 %all-gather.45.cloned.1.call-start = ((), (), s32[]{:S(2)}) async-start(), calls=%async_computation.55 | async-start | bytes 2359296 | tf_op jit(solution)/shard_map/all_gather | solution.py:140
  43.6 169.8 %reduce-scatter.25.cloned.1.call-start = ((), (), s32[]{:S(2)}) async-start(), calls=%async_computation.28 | async-start | bytes 3932160 | tf_op jit(solution)/shard_map/reduce_scatter | solution.py:60
  154.7 187.6 %all-gather.29.cloned.1.call-start = ((), (), s32[]{:S(2)}) async-start(), calls=%async_computation.29 | async-start | bytes 3932160 | tf_op jit(solution)/shard_map/all_gather | solution.py:52
  216.5 147.4 %all-gather.47.cloned.1.call-start = ((), (), s32[]{:S(2)}) async-start(), calls=%async_computation.56 | async-start | bytes 9437184 | tf_op jit(solution)/shard_map/all_gather | solution.py:142
  227.4 114.9 %all-to-all-start.2 = ((bf16[8,256,2048]{2,1,0:T(8,128)(2,1)}), bf16[8,256,2048]{2,1,0:T(8,128)(2,1)}, u32[]{:S(2)}, u32[]{:S(2)}) async-start(bf16[8,256,2048]{2,1,0:T(8,128)(2,1)} %stack.147), calls=%async_computation.3 | async-start | bytes 16777216 | tf_op jit(solution)/shard_map/all_to_all | solution.py:12
  232.6 203.1 %reduce-scatter.27.cloned.1.call-start = ((), (), s32[]{:S(2)}) async-start(), calls=%async_computation.30 | async-start | bytes 3932160 | tf_op jit(solution)/shard_map/reduce_scatter | solution.py:60
  243.9 584.6 %copy-start.95 = (f32[1,2048]{1,0:T(1,128)}, f32[1,2048]{1,0:T(1,128)S(1)}, u32[]{:S(2)}) copy-start(f32[1,2048]{1,0:T(1,128)S(1)} %get-tuple-element.587) | copy-start | bytes 24580
  377.0 88.5 %all-gather.49.cloned.1.call-start = ((), (), s32[]{:S(2)}) async-start(), calls=%async_computation.57 | async-start | bytes 2359296 | tf_op jit(solution)/shard_map/all_gather | solution.py:138
  377.8 153.4 %all-gather.31.cloned.1.call-start = ((), (), s32[]{:S(2)}) async-start(), calls=%async_computation.31 | async-start | bytes 3932160 | tf_op jit(solution)/shard_map/all_gather | solution.py:52
  438.7 138.0 %all-gather.51.cloned.1.call-start = ((), (), s32[]{:S(2)}) async-start(), calls=%async_computation.58 | async-start | bytes 2359296 | tf_op jit(solution)/shard_map/all_gather | solution.py:140
  439.3 201.2 %reduce-scatter.29.cloned.1.call-start = ((), (), s32[]{:S(2)}) async-start(), calls=%async_computation.32 | async-start | bytes 3932160 | tf_op jit(solution)/shard_map/reduce_scatter | solution.py:60
  582.0 181.4 %all-gather.33.cloned.1.call-start = ((), (), s32[]{:S(2)}) async-start(), calls=%async_computation.33 | async-start | bytes 3932160 | tf_op jit(solution)/shard_map/all_gather | solution.py:52
  641.9 317.5 %copy-start.6 = (f32[192,2048]{1,0:T(8,128)}, f32[192,2048]{1,0:T(8,128)S(1)}, u32[]{:S(2)}) copy-start(f32[192,2048]{1,0:T(8,128)S(1)} %get-tuple-element.556) | copy-start | bytes 4718596
  643.6 131.5 %all-gather.35.cloned.1.call-start = ((), (), s32[]{:S(2)}) async-start(), calls=%async_computation.35 | async-start | bytes 3932160 | tf_op jit(solution)/shard_map/all_gather | solution.py:56
  661.9 298.2 %copy-start.17 = (f32[192,2048]{1,0:T(8,128)}, f32[192,2048]{1,0:T(8,128)S(1)}, u32[]{:S(2)}) copy-start(f32[192,2048]{1,0:T(8,128)S(1)} %get-tuple-element.607) | copy-start | bytes 4718596
  661.9 166.6 %all-gather.53.cloned.1.call-start = ((), (), s32[]{:S(2)}) async-start(), calls=%async_computation.59 | async-start | bytes 9437184 | tf_op jit(solution)/shard_map/all_gather | solution.py:142
  662.5 222.2 %all-gather.55.cloned.1.call-start = ((), (), s32[]{:S(2)}) async-start(), calls=%async_computation.60 | async-start | bytes 9437184 | tf_op jit(solution)/shard_map/all_gather | solution.py:212
  663.1 293.9 %reduce-scatter.33.cloned.1.call-start = ((), (), s32[]{:S(2)}) async-start(), calls=%async_computation.36 | async-start | bytes 3932160 | tf_op jit(solution)/shard_map/reduce_scatter | solution.py:70
  896.6 129.1 %all-gather.37.cloned.1.call-start = ((), (), s32[]{:S(2)}) async-start(), calls=%async_computation.37 | async-start | bytes 3932160 | tf_op jit(solution)/shard_map/all_gather | solution.py:56
  962.1 135.1 %reduce-scatter.61.cloned.1.call-start = ((), (), s32[]{:S(2)}) async-start(), calls=%async_computation.62 | async-start | bytes 491520
  1077.8 83.6 %reduce-scatter.35.cloned.1.call-start = ((), (), s32[]{:S(2)}) async-start(), calls=%async_computation.38 | async-start | bytes 3932160 | tf_op jit(solution)/shard_map/reduce_scatter | solution.py:70
  1102.8 130.1 %all-gather.39.cloned.1.call-start = ((), (), s32[]{:S(2)}) async-start(), calls=%async_computation.39 | async-start | bytes 3932160 | tf_op jit(solution)/shard_map/all_gather | solution.py:56
  1169.2 118.8 %all-gather.57.cloned.1.call-start = ((), (), s32[]{:S(2)}) async-start(), calls=%async_computation.61 | async-start | bytes 9437184 | tf_op jit(solution)/shard_map/all_gather | solution.py:212
  1169.9 188.7 %reduce-scatter.37.cloned.1.call-start = ((), (), s32[]{:S(2)}) async-start(), calls=%async_computation.40 | async-start | bytes 3932160 | tf_op jit(solution)/shard_map/reduce_scatter | solution.py:70
  1298.3 129.5 %all-gather.41.cloned.1.call-start = ((), (), s32[]{:S(2)}) async-start(), calls=%async_computation.41 | async-start | bytes 3932160 | tf_op jit(solution)/shard_map/all_gather | solution.py:56
  1364.0 134.4 %reduce-scatter.63.cloned.1.call-start = ((), (), s32[]{:S(2)}) async-start(), calls=%async_computation.63 | async-start | bytes 491520
  1479.0 93.3 %reduce-scatter.31.cloned.1.call-start = ((), (), s32[]{:S(2)}) async-start(), calls=%async_computation.34 | async-start | bytes 3932160 | tf_op jit(solution)/shard_map/reduce_scatter | solution.py:60
  1492.2 191.3 %all-reduce.7.cloned.1.call-start = ((), (), s32[]{:S(2)}) async-start(), calls=%async_computation.51 | async-start | bytes 131072 | tf_op jit(solution)/shard_map/psum | solution.py:322
  1493.6 227.2 %reduce-scatter.47.cloned.1.call-start = ((), (), s32[]{:S(2)}) async-start(), calls=%async_computation.46 | async-start | bytes 294912 | tf_op jit(solution)/shard_map/reduce_scatter | solution.py:291
  1497.0 260.8 %reduce-scatter.45.cloned.1.call-start = ((), (), s32[]{:S(2)}) async-start(), calls=%async_computation.45 | async-start | bytes 294912 | tf_op jit(solution)/shard_map/reduce_scatter | solution.py:291
  1500.7 331.8 %reduce-scatter.55.cloned.1.call-start = ((), (), s32[]{:S(2)}) async-start(), calls=%async_computation.50 | async-start | bytes 9437184 | tf_op jit(solution)/shard_map/reduce_scatter | solution.py:297
  1512.3 395.2 %reduce-scatter.53.cloned.1.call-start = ((), (), s32[]{:S(2)}) async-start(), calls=%async_computation.49 | async-start | bytes 9437184 | tf_op jit(solution)/shard_map/reduce_scatter | solution.py:297
  1524.0 446.1 %reduce-scatter.39.cloned.1.call-start = ((), (), s32[]{:S(2)}) async-start(), calls=%async_computation.42 | async-start | bytes 3932160 | tf_op jit(solution)/shard_map/reduce_scatter | solution.py:70
  1530.5 514.5 %reduce-scatter.59.cloned.1.call-start = ((), (), s32[]{:S(2)}) async-start(), calls=%async_computation.53 | async-start | bytes 9437184 | tf_op jit(solution)/shard_map/reduce_scatter | solution.py:300
  1543.5 576.5 %reduce-scatter.57.cloned.1.call-start = ((), (), s32[]{:S(2)}) async-start(), calls=%async_computation.52 | async-start | bytes 9437184 | tf_op jit(solution)/shard_map/reduce_scatter | solution.py:300
  1556.8 607.7 %reduce-scatter.43.cloned.1.call-start = ((), (), s32[]{:S(2)}) async-start(), calls=%async_computation.44 | async-start | bytes 2359296 | tf_op jit(solution)/shard_map/reduce_scatter | solution.py:288
  1562.2 647.2 %reduce-scatter.41.cloned.1.call-start = ((), (), s32[]{:S(2)}) async-start(), calls=%async_computation.43 | async-start | bytes 2359296 | tf_op jit(solution)/shard_map/reduce_scatter | solution.py:288
  1566.6 687.2 %reduce-scatter.51.cloned.1.call-start = ((), (), s32[]{:S(2)}) async-start(), calls=%async_computation.48 | async-start | bytes 2359296 | tf_op jit(solution)/shard_map/reduce_scatter | solution.py:294
  1576.1 16.4 all-to-all-start.4
  1579.9 718.7 %reduce-scatter.49.cloned.1.call-start = ((), (), s32[]{:S(2)}) async-start(), calls=%async_computation.47 | async-start | bytes 2359296 | tf_op jit(solution)/shard_map/reduce_scatter | solution.py:294
  1975.8 457.9 %all-to-all-start.6 = ((bf16[8,24,2048]{2,1,0:T(8,128)(2,1)}), bf16[8,24,2048]{2,1,0:T(8,128)(2,1)S(1)}, u32[]{:S(2)}, u32[]{:S(2)}) async-start(bf16[8,24,2048]{2,1,0:T(8,128)(2,1)} %bitcast.341), calls=%async_computation.14 | async-start | bytes 1572864 | tf_op jit(solution)/shard_map/all_to_all | solution.py:345
  1979.5 451.7 %all-reduce.9.cloned.1.call-start = ((), (), s32[]{:S(2)}) async-start(), calls=%async_computation.64 | async-start | bytes 233472 | tf_op jit(solution)/shard_map/psum | solution.py:322
  (120 other events, 3420.4 us)
Sparse Core Ops, SparseCore 0:
  10.5 33.2 all-gather.42
  46.0 63.7 all-gather.26
  112.2 26.8 all-gather.44
  154.8 58.5 reduce-scatter.24
  216.6 63.5 all-gather.28
  282.5 81.3 all-gather.46
  377.1 58.4 reduce-scatter.26
  437.5 27.9 all-gather.48
  467.6 63.4 all-gather.30
  532.9 26.8 all-gather.50
  582.2 58.3 reduce-scatter.28
  643.7 63.5 all-gather.32
  709.4 62.1 all-gather.34
  773.9 54.5 all-gather.52
  830.2 54.3 all-gather.54
  896.7 60.2 reduce-scatter.32
  962.2 63.5 all-gather.36
  1077.9 19.2 reduce-scatter.60
  1102.9 58.5 reduce-scatter.34
  1169.3 63.4 all-gather.38
  1234.9 53.0 all-gather.56
  1298.4 60.2 reduce-scatter.36
  1364.2 63.5 all-gather.40
  1479.1 19.2 reduce-scatter.62
  1501.3 58.5 reduce-scatter.30
  1565.9 117.5 all-reduce.6
  1686.3 34.4 reduce-scatter.46
  1724.1 33.5 reduce-scatter.44
  1761.2 71.2 reduce-scatter.54
  1836.2 71.2 reduce-scatter.52
  1909.9 60.2 reduce-scatter.38
  1973.6 71.3 reduce-scatter.58
  2048.7 71.2 reduce-scatter.56
  2123.3 41.2 reduce-scatter.42
  2168.2 41.2 reduce-scatter.40
  2212.6 41.2 reduce-scatter.50
  2257.3 41.2 reduce-scatter.48
  2306.1 125.0 all-reduce.8
